TPU v7x, 32 devices: a whole 2x2x4 slice. The times are simulated.
32 devices in a mesh: layer: 4 (over y, x), lat: 8 (over z, core).
Axes of the slice: x: 2, y: 2, z: 4, core: 2. Of those that a mesh axis runs over, the one named last changes fastest.
Arguments:
- inputs: bfloat16 [4, 1, 5120, 128], P(None, None, 'lat'), may hold values from -6 to 6
- encoder: bfloat16 [4, 8192, 5120], P('layer', 'lat'), may hold values from -0.125 to 0.125
- decoder: bfloat16 [4, 4, 8192, 5120], P('layer', None, 'lat'), may hold values from -0.09375 to 0.09375
- encoder_bias: float32 [4, 8192], P(None, 'lat'), may hold values from -3 to 3
- tile_mask: int32 [4, 64, 128], P(None, 'lat'), may hold values 0 or 1
- targets: bfloat16 [1, 5120, 4, 128], P(None, 'lat'), may hold values from -6 to 6
- decoder_bias: float32 [1, 5120, 4], P(None, 'lat'), may hold values from -3 to 3
Outputs:
- errors: bfloat16 [1, 5120, 4, 128], P(None, 'lat')
- input_grads: bfloat16 [4, 5120, 128], P('layer', 'lat')
All inputs are finite; a program needn't handle non-finite values. No bound on the sum of `tile_mask` on one device may be relied on, other than what follows from the above.
Results may differ from a plain program's by a relative error of at most 0.0065.
Values may be sent and summed in bfloat16 or wider, within the bound.
A program may use at most 192 MiB of HBM per device.

v0:
```python
import jax
import jax.numpy as jnp
from jax import lax
from jax.sharding import PartitionSpec as P

TILE = 128


def over_sources(values):
    return lax.psum(values, "layer")


def run_blocks(totals, source_row, blocks, base_target, low_target, high_target, update):

    def advance(target, current):
        weights = lax.dynamic_index_in_dim(blocks, target - base_target, 0, keepdims=False)
        return update(current, target, source_row, weights)

    return lax.fori_loop(low_target, high_target, advance, totals)


def per_device(inputs, encoder, decoder, encoder_bias, tile_mask, targets, decoder_bias):
    layer_count = lax.axis_size("layer")
    lat_count = lax.axis_size("lat")
    layers = decoder.shape[1]
    quarters = layer_count // layers
    position = lax.axis_index("layer")
    source = position // quarters
    quarter = position % quarters
    encoder_rows = encoder[0]
    own_blocks = decoder[0]
    local_latents = encoder_rows.shape[0]
    quarter_width = encoder_rows.shape[1]
    kept_width = quarter_width // lat_count
    row_count = inputs.shape[3]
    block_jobs = [(source, own_blocks, 0, source, layers)]

    def run_all(totals, update):
        block_job = block_jobs[0]
        totals = run_blocks(
            totals, block_job[0], block_job[1], block_job[2], block_job[3], block_job[4], update
        )
        return totals

    own_input = lax.dynamic_index_in_dim(
        inputs.reshape((layers * quarters,) + inputs.shape[2:]), position, 0, keepdims=False
    )
    full_input = lax.all_gather(own_input, "lat", axis=0, tiled=True)
    own_preacts = jnp.dot(encoder_rows, full_input, preferred_element_type=jnp.float32)
    tile_count = tile_mask.shape[1]
    support = jnp.broadcast_to(
        tile_mask[:, :, None, :].astype(jnp.float32), (layers, tile_count, TILE, row_count)
    ).reshape(layers, local_latents, row_count)
    own_support = lax.dynamic_index_in_dim(support, source, 0, keepdims=False)
    source_slots = lax.dynamic_update_index_in_dim(
        jnp.zeros((layers, local_latents, row_count), jnp.float32), own_preacts, source, 0
    )
    preacts = over_sources(source_slots) + encoder_bias[:, :, None]
    activity = (jnp.maximum(preacts, 0.0) * support).astype(jnp.bfloat16)

    def forward_term():

        def update(current, target, source_row, weights):
            latent = lax.dynamic_index_in_dim(activity, source_row, 0, keepdims=False)
            contrib = lax.dot_general(
                weights, latent, (((0,), (0,)), ((), ())), preferred_element_type=jnp.float32
            )
            before = lax.dynamic_index_in_dim(current, target, 1, keepdims=False)
            return lax.dynamic_update_index_in_dim(current, before + contrib, target, 1)

        return run_all(
            jnp.zeros((kept_width * lax.axis_size("lat"), layers, row_count), jnp.float32), update
        )

    partial_value = lax.psum_scatter(forward_term(), "lat", scatter_dimension=0, tiled=True)
    placed = lax.dynamic_update_index_in_dim(
        jnp.zeros((quarters,) + partial_value.shape, jnp.float32), partial_value, quarter, 0
    )
    summed = over_sources(placed)
    errors = (summed + decoder_bias[:, :, :, None] - targets.astype(jnp.float32)).astype(
        jnp.bfloat16
    )
    own_errors = lax.dynamic_index_in_dim(errors, quarter, 0, keepdims=False)

    def fold_errors(totals, portion):

        def update(current, target, source_row, weights):
            error_rows = lax.dynamic_index_in_dim(portion, target, 1, keepdims=False)
            contrib = jnp.dot(weights, error_rows, preferred_element_type=jnp.float32)
            before = lax.dynamic_index_in_dim(current, source_row, 0, keepdims=False)
            return lax.dynamic_update_index_in_dim(current, before + contrib, source_row, 0)

        return run_all(totals, update)

    latent_sums = fold_errors(
        jnp.zeros((layers, local_latents, row_count), jnp.float32),
        lax.all_gather(own_errors, "lat", axis=0, tiled=True),
    )
    latent_grad = over_sources(latent_sums)
    own_latent = lax.dynamic_index_in_dim(latent_grad, source, 0, keepdims=False)
    own_grad = (own_latent * own_support).astype(jnp.bfloat16)
    gradients = lax.psum_scatter(
        lax.dot_general(
            encoder_rows, own_grad, (((0,), (0,)), ((), ())), preferred_element_type=jnp.float32
        ),
        "lat",
        scatter_dimension=0,
        tiled=True,
    )
    return (errors, gradients.astype(jnp.bfloat16)[None])


def solution(mesh):
    in_specs = (
        P(None, None, "lat", None),
        P("layer", "lat", None),
        P("layer", None, "lat", None),
        P(None, "lat"),
        P(None, "lat", None),
        P(None, "lat", None, None),
        P(None, "lat", None),
    )
    out_specs = (P(None, "lat", None, None), P("layer", "lat", None))
    return jax.shard_map(
        per_device, mesh=mesh, in_specs=in_specs, out_specs=out_specs, check_vma=False
    )
```

profile of v0, /device:TPU:0, one launch (start us, length us, event | category | flops | bytes accessed | tf_op | source)
XLA Modules:
  0.0 923.1 jit_solution(17247908552409753957)
XLA Ops:
  7.2 0.0 copy-start
  7.2 0.0 all-gather.5.cloned.1.call-start
  7.2 1.0 copy-done
  8.3 0.7 constant_dynamic-slice_fusion.3
  8.9 0.0 all-gather.5.cloned.1.call-update
  9.0 0.0 all-reduce.6.cloned.1.call-start
  9.0 27.4 %all-gather.5.cloned.1.call-done = bf16[1,1,5120,128]{3,2,1,0:T(8,128)(2,1)} async-done(((bf16[1,1,640,128]{3,2,1,0:T(8,128)(2,1)}), bf16[1,1,5120,128]{3,2,1,0:T(8,128)(2,1)}) %all-gather.5.cloned.1.call-update) | async-done | bytes 1310736 | tf_op jit(solution)/shard_map/all_gather | solution.py:48
  36.4 8.0 fusion.37
  44.4 0.2 copy.18
  44.6 0.0 copy-start.6
  44.6 0.1 broadcast.8.clone
  44.8 1.3 copy-done.3
  46.1 0.0 all-reduce.6.cloned.1.call-update
  46.1 0.0 all-reduce.12.cloned.1.call-start
  46.2 0.7 constant_dynamic-slice_fusion.2
  46.9 68.4 %all-reduce.6.cloned.1.call-done = f32[4,1024,128]{2,1,0:T(8,128)} async-done(((f32[4,1024,128]{2,1,0:T(8,128)}), f32[4,1024,128]{2,1,0:T(8,128)}) %all-reduce.6.cloned.1.call-update) | async-done | bytes 2097168 | tf_op jit(solution)/shard_map/psum | solution.py:10
  115.3 0.1 broadcast_in_dim.37
  115.4 1.3 copy-done.4
  116.8 1.2 fusion.44
  118.0 4.8 broadcast_in_dim.35.clone
  122.8 315.8 %while.24 = (s32[]{:T(128)}, f32[5120,4,128]{2,1,0:T(4,128)}, bf16[4,1024,5120]{2,1,0:T(8,128)(2,1)}, bf16[1,1024,128]{2,1,0:T(8,128)(2,1)S(1)}, s32[]{:T(128)}, /*index=5*/s32[]{:T(128)}, s32[]{:T(128)}) while((s32[]{:T(128)}, f32[5120,4,128]{2,1,0:T(4,128)}, bf16[4,1024,5120]{2,1,0:T(8,128)(2,1)}, bf16[1,1024,128]{2,1,0:T(8,128)(2,1)S(1)}, ...), condition=%wide.region_2.3_spmd, body=%wide.region_1.2_spmd.sunk | while | flops 1342832640 | bytes 26476668 | solution.py:19
  122.8 6.3 constant_dynamic-slice_fusion.6
  129.1 5.8 fusion.56
  134.8 66.9 %dynamic_update_slice.23 = f32[5120,4,128]{2,1,0:T(4,128)} dynamic-update-slice(f32[5120,4,128]{2,1,0:T(4,128)} %get-tuple-element.226, f32[5120,1,128]{2,1,0:T(1,128)S(1)} %bitcast.87, s32[]{:T(128)} %constant.114.clone.1..sunk, s32[]{:T(128)S(6)} %select_n.50, s32[]{:T(128)} %constant.114.clone.1..sunk) | dynamic-update-slice | bytes 5242884 | tf_op jit(solution)/shard_map/while/body/jit(dynamic_update_index_in_dim)/dynamic_update_slice | solution.py:69
  201.7 6.3 constant_dynamic-slice_fusion.6
  208.0 5.8 fusion.56
  213.8 66.9 %dynamic_update_slice.23 = f32[5120,4,128]{2,1,0:T(4,128)} dynamic-update-slice(f32[5120,4,128]{2,1,0:T(4,128)} %get-tuple-element.226, f32[5120,1,128]{2,1,0:T(1,128)S(1)} %bitcast.87, s32[]{:T(128)} %constant.114.clone.1..sunk, s32[]{:T(128)S(6)} %select_n.50, s32[]{:T(128)} %constant.114.clone.1..sunk) | dynamic-update-slice | bytes 5242884 | tf_op jit(solution)/shard_map/while/body/jit(dynamic_update_index_in_dim)/dynamic_update_slice | solution.py:69
  280.7 6.3 constant_dynamic-slice_fusion.6
  287.0 5.8 fusion.56
  292.7 66.9 %dynamic_update_slice.23 = f32[5120,4,128]{2,1,0:T(4,128)} dynamic-update-slice(f32[5120,4,128]{2,1,0:T(4,128)} %get-tuple-element.226, f32[5120,1,128]{2,1,0:T(1,128)S(1)} %bitcast.87, s32[]{:T(128)} %constant.114.clone.1..sunk, s32[]{:T(128)S(6)} %select_n.50, s32[]{:T(128)} %constant.114.clone.1..sunk) | dynamic-update-slice | bytes 5242884 | tf_op jit(solution)/shard_map/while/body/jit(dynamic_update_index_in_dim)/dynamic_update_slice | solution.py:69
  359.6 6.3 constant_dynamic-slice_fusion.6
  365.9 5.8 fusion.56
  371.7 66.9 %dynamic_update_slice.23 = f32[5120,4,128]{2,1,0:T(4,128)} dynamic-update-slice(f32[5120,4,128]{2,1,0:T(4,128)} %get-tuple-element.226, f32[5120,1,128]{2,1,0:T(1,128)S(1)} %bitcast.87, s32[]{:T(128)} %constant.114.clone.1..sunk, s32[]{:T(128)S(6)} %select_n.50, s32[]{:T(128)} %constant.114.clone.1..sunk) | dynamic-update-slice | bytes 5242884 | tf_op jit(solution)/shard_map/while/body/jit(dynamic_update_index_in_dim)/dynamic_update_slice | solution.py:69
  438.6 0.0 all-reduce.12.cloned.1.call-update
  438.6 0.0 copy-start.5
  438.6 0.0 all-reduce.8.cloned.1.call-start
  438.7 0.6 copy-done.8
  439.2 0.6 dynamic-slice.1
  440.5 212.4 %all-reduce.12.cloned.1.call-done = f32[5120,4,128]{2,1,0:T(4,128)} async-done(((f32[5120,4,128]{2,1,0:T(4,128)}), f32[5120,4,128]{2,1,0:T(4,128)}) %all-reduce.12.cloned.1.call-update) | async-done | bytes 10485776
  652.9 2.5 dynamic-slice_bitcast_fusion
  655.3 0.0 all-reduce.8.cloned.1.call-update
  655.4 0.0 all-gather.7.cloned.1.call-start
  655.4 0.2 copy.20
  655.6 56.7 %all-reduce.8.cloned.1.call-done = f32[1,640,4,128]{3,2,1,0:T(4,128)} async-done(((f32[1,640,4,128]{3,2,1,0:T(4,128)}), f32[1,640,4,128]{3,2,1,0:T(4,128)}) %all-reduce.8.cloned.1.call-update) | async-done | bytes 1310736 | tf_op jit(solution)/shard_map/psum | solution.py:10
  712.3 2.6 subtract_convert_fusion
  715.0 0.0 all-gather.7.cloned.1.call-update
  715.0 0.0 all-reduce.10.cloned.1.call-start
  715.1 56.1 %all-gather.7.cloned.1.call-done = bf16[1,5120,4,128]{3,2,0,1:T(4,128)(2,1)} async-done(((bf16[1,640,4,128]{3,2,0,1:T(4,128)(2,1)}), bf16[1,5120,4,128]{3,2,0,1:T(4,128)(2,1)}) %all-gather.7.cloned.1.call-update) | async-done | bytes 5242896 | tf_op jit(solution)/shard_map/all_gather | solution.py:97
  771.1 5.5 copy.22
  776.6 0.1 broadcast.8
  776.7 24.3 %while.25 = (s32[]{:T(128)}, f32[4,1024,128]{2,1,0:T(8,128)S(1)}, s32[]{:T(128)}, bf16[4,1024,5120]{2,1,0:T(8,128)(2,1)}, bf16[5120,4,128]{2,0,1:T(8,128)(2,1)}, /*index=5*/s32[]{:T(128)}, s32[]{:T(128)}, s32[]{:T(128)}) while((s32[]{:T(128)}, f32[4,1024,128]{2,1,0:T(8,128)S(1)}, s32[]{:T(128)}, bf16[4,1024,5120]{2,1,0:T(8,128)(2,1)}, ...), condition=%wide.region_6.7_spmd, body=%wide.region_5.6_spmd.sunk | while | flops 1342308352 | bytes 13895291 | solution.py:19
  776.8 6.0 fusion.59
  782.9 6.0 fusion.59
  789.0 6.0 fusion.59
  795.1 6.0 fusion.59
  801.1 1.3 copy-done.2
  802.4 0.0 all-reduce.10.cloned.1.call-update
  802.5 0.0 reduce-scatter.2.cloned.1.call-start
  802.5 66.5 %all-reduce.10.cloned.1.call-done = f32[4,1024,128]{2,1,0:T(8,128)} async-done(((f32[4,1024,128]{2,1,0:T(8,128)}), f32[4,1024,128]{2,1,0:T(8,128)}) %all-reduce.10.cloned.1.call-update) | async-done | bytes 2097168 | tf_op jit(solution)/shard_map/psum | solution.py:10
  869.0 7.4 fusion.33
  876.5 0.0 reduce-scatter.2.cloned.1.call-update
  876.5 38.0 %reduce-scatter.2.cloned.1.call-done = f32[640,128]{0,1:T(8,128)} async-done(((f32[5120,128]{0,1:T(8,128)}), f32[640,128]{0,1:T(8,128)}) %reduce-scatter.2.cloned.1.call-update) | async-done | bytes 327696 | tf_op jit(solution)/shard_map/reduce_scatter | solution.py:102
  914.5 1.0 convert_bitcast_fusion
  915.5 0.8 copy.23
  (16 shorter events, 0.2 us)
Async XLA Ops:
  7.2 1.1 copy-start
  7.2 29.2 %all-gather.5.cloned.1.call-start = ((), (), s32[]{:S(2)}) async-start(), calls=%async_computation.5 | async-start | bytes 1474560 | tf_op jit(solution)/shard_map/all_gather | solution.py:48
  9.0 106.3 %all-reduce.6.cloned.1.call-start = ((), (), s32[]{:S(2)}) async-start(), calls=%async_computation.1 | async-start | bytes 4194304 | tf_op jit(solution)/shard_map/psum | solution.py:10
  44.6 1.6 copy-start.6
  44.8 1.3 copy-start.3
  46.1 606.8 %all-reduce.12.cloned.1.call-start = ((), (), s32[]{:S(2)}) async-start(), calls=%async_computation.7 | async-start | bytes 20971520
  115.4 1.4 copy-start.4
  438.6 0.7 copy-start.8
  438.6 216.8 %copy-start.7 = (f32[1,640,4]{1,2,0:T(4,128)S(1)}, f32[1,640,4]{1,2,0:T(4,128)}, u32[]{:S(2)}) copy-start(f32[1,640,4]{1,2,0:T(4,128)} %param.17) | copy-start | bytes 30724
  438.6 273.7 %copy-start.5 = (bf16[1,640,4,128]{3,2,1,0:T(4,128)(2,1)S(1)}, bf16[1,640,4,128]{3,2,1,0:T(4,128)(2,1)}, u32[]{:S(2)}) copy-start(bf16[1,640,4,128]{3,2,1,0:T(4,128)(2,1)} %param.16) | copy-start | bytes 1966084
  438.6 273.7 %all-reduce.8.cloned.1.call-start = ((), (), s32[]{:S(2)}) async-start(), calls=%async_computation.2 | async-start | bytes 2621440 | tf_op jit(solution)/shard_map/psum | solution.py:10
  655.4 115.8 %all-gather.7.cloned.1.call-start = ((), (), s32[]{:S(2)}) async-start(), calls=%async_computation.6 | async-start | bytes 5898240 | tf_op jit(solution)/shard_map/all_gather | solution.py:97
  715.0 154.0 %all-reduce.10.cloned.1.call-start = ((), (), s32[]{:S(2)}) async-start(), calls=%async_computation.3 | async-start | bytes 4194304 | tf_op jit(solution)/shard_map/psum | solution.py:10
  801.1 1.3 copy-start.2
  802.5 112.0 %reduce-scatter.2.cloned.1.call-start = ((), (), s32[]{:S(2)}) async-start(), calls=%async_computation.4 | async-start | bytes 2949120 | tf_op jit(solution)/shard_map/reduce_scatter | solution.py:102
  869.0 47.3 %copy-start.1 = (bf16[4,1,640,128]{3,2,1,0:T(8,128)(2,1)S(1)}, bf16[4,1,640,128]{3,2,1,0:T(8,128)(2,1)}, u32[]{:S(2)}) copy-start(bf16[4,1,640,128]{3,2,1,0:T(8,128)(2,1)} %param.11) | copy-start | bytes 1966084
Sparse Core Ops, SparseCore 0:
  10.2 26.1 all-gather.4
  46.2 68.9 all-reduce.5
  438.7 214.1 all-reduce.11
  655.8 56.4 all-reduce.7
  715.1 55.9 all-gather.6
  802.6 66.3 all-reduce.9
  876.6 37.8 reduce-scatter.1
where the time goes:
time: 930 us; the launch traced here: 923 us
  waiting for transfers between devices  526 us (57%)
  local copies, waits for them, and re-layouts  315 us (34%)
  matrix products  62.5 us (7%)
  between operations  14.9 us (2%)
    dynamic_update_slice x4, local copies, waits for them, and re-layouts, update(): return lax.dynamic_update_index_in_dim(current, before + contrib, target, 1)  268 us
    unnamed x8, waiting for transfers between devices  213 us
    psum x3, waiting for transfers between devices, over_sources(): return lax.psum(values, 'layer')  192 us
    all_gather x1, waiting for transfers between devices, per_device(): lax.all_gather(own_errors, 'lat', axis=0, tiled=True)  56.1 us
    reduce_scatter x1, waiting for transfers between devices, per_device(): lax.psum_scatter(lax.dot_general(encoder_rows, own_grad, (((0,), (0,)), (...  38 us
    all_gather x1, waiting for transfers between devices, per_device(): full_input = lax.all_gather(own_input, 'lat', axis=0, tiled=True)  27.4 us
    dynamic_slice x4, local copies, waits for them, and re-layouts, update(): before = lax.dynamic_index_in_dim(current, target, 1, keepdims=False)  25 us
    dot_general x4, matrix products, update(): contrib = jnp.dot(weights, error_rows, preferred_element_type=jnp.float32)  24 us
  transfers between devices with their start and end apart: 7, of which 7 were waited for; matrix products, arithmetic and copies ran while one was open for 0% of the time, Pallas kernels for 0%

commit v1 on v0

--- a/solution.py
+++ b/solution.py
@@ -7,7 +7,8 @@
 
 
 def over_sources(values):
-    return lax.psum(values, "layer")
+    find_leaf = lambda vals, which_axis: jnp.sum(lax.all_gather(vals, which_axis), axis=0)
+    return find_leaf(values, "layer")
 
 
 def run_blocks(totals, source_row, blocks, base_target, low_target, high_target, update):

time: 930 us -> 591 us (0.64)
  local copies, waits for them, and re-layouts: 315 us -> 30 us
  waiting for transfers between devices: 526 us -> 459 us
  matrix products: 62.5 us -> 73.3 us
    dynamic_update_slice x4 -> x0, local copies, waits for them, and re-layouts: 268 us -> none  [update(): return lax.dynamic_update_index_in_dim(current, before + contrib, target, 1)]
    all_gather x0 -> x3, waiting for transfers between devices: none -> 230 us  [over_sources(): lax.all_gather(vals, which_axis)]
    unnamed x8 -> x7, waiting for transfers between devices: 213 us -> 0.11 us
    psum x3 -> x0, waiting for transfers between devices: 192 us -> none  [over_sources(): return lax.psum(values, 'layer')]
    reduce_scatter x0 -> x1, waiting for transfers between devices: none -> 109 us  [per_device(): lax.psum_scatter(forward_term(), 'lat', scatter_dimension=0, tiled=True)]
    dynamic_slice x4, local copies, waits for them, and re-layouts: 25 us -> 7.63 us  [update(): before = lax.dynamic_index_in_dim(current, target, 1, keepdims=False)]
    reduce_sum x0 -> x3, other arithmetic: none -> 11.2 us  [over_sources(): jnp.sum(lax.all_gather(vals, which_axis), axis=0)]
    dot_general x4, matrix products: 23 us -> 34 us  [update(): lax.dot_general(weights, latent, (((0,), (0,)), ((), ())), preferred_elem...]
  transfers between devices with their start and end apart: 7 -> 7, of which waited for: 7 -> 7; matrix products, arithmetic and copies ran while one was open for 0% -> 1% of each run, Pallas kernels for 0% -> 0%
where the time goes in v1:
time: 591 us
  waiting for transfers between devices  459 us (78%)
  matrix products  73.3 us (12%)
  local copies, waits for them, and re-layouts  30 us (5%)
  between operations  14.3 us (2%)
  other arithmetic  13.8 us (2%)
    all_gather x3, waiting for transfers between devices, over_sources(): lax.all_gather(vals, which_axis)  230 us
    reduce_scatter x1, waiting for transfers between devices, per_device(): lax.psum_scatter(forward_term(), 'lat', scatter_dimension=0, tiled=True)  109 us
    all_gather x1, waiting for transfers between devices, per_device(): lax.all_gather(own_errors, 'lat', axis=0, tiled=True)  55.9 us
    reduce_scatter x1, waiting for transfers between devices, per_device(): lax.psum_scatter(lax.dot_general(encoder_rows, own_grad, (((0,), (0,)), (...  36.6 us
    dot_general x4, matrix products, update(): lax.dot_general(weights, latent, (((0,), (0,)), ((), ())), preferred_elem...  34 us
    all_gather x1, waiting for transfers between devices, per_device(): full_input = lax.all_gather(own_input, 'lat', axis=0, tiled=True)  27.4 us
    dot_general x4, matrix products, update(): contrib = jnp.dot(weights, error_rows, preferred_element_type=jnp.float32)  24 us
  transfers between devices with their start and end apart: 7, of which 7 were waited for; matrix products, arithmetic and copies ran while one was open for 1% of the time, Pallas kernels for 0%

profile of v1, /device:TPU:0, one launch (start us, length us, event | category | flops | bytes accessed | tf_op | source)
XLA Modules:
  0.0 590.6 jit_solution(9620101383938846342)
XLA Ops:
  7.2 0.0 copy-start
  7.2 0.0 all-gather.12.cloned.1.call-start
  7.2 1.0 copy-done
  8.3 0.7 constant_dynamic-slice_fusion.5
  8.9 0.0 all-gather.12.cloned.1.call-update
  9.0 0.0 all-gather.10.cloned.1.call-start
  9.0 27.4 %all-gather.12.cloned.1.call-done = bf16[1,1,5120,128]{3,2,1,0:T(8,128)(2,1)} async-done(((bf16[1,1,640,128]{3,2,1,0:T(8,128)(2,1)}), bf16[1,1,5120,128]{3,2,1,0:T(8,128)(2,1)}) %all-gather.12.cloned.1.call-update) | async-done | bytes 1310736 | tf_op jit(solution)/shard_map/all_gather | solution.py:49
  36.4 8.0 %fusion.45 = f32[1,1,1024,128]{2,3,1,0:T(8,128)S(1)} fusion(bf16[1,1024,5120]{2,1,0:T(8,128)(2,1)} %param.12, bf16[1,1,5120,128]{3,2,1,0:T(8,128)(2,1)} %all-gather.12.cloned.1.call-done), kind=kOutput, calls=%fused_computation.28 | convolution fusion | flops 1342177280 | bytes 12320768 | tf_op jit(solution)/shard_map/dot_general | solution.py:50
  44.4 0.2 copy.24
  44.6 0.0 copy-start.5
  44.6 0.1 all_gather.26
  44.8 1.4 copy-done.3
  46.2 0.0 all-gather.10.cloned.1.call-update
  46.2 0.0 reduce-scatter.3.cloned.1.call-start
  46.2 0.1 copy.26
  46.4 0.6 broadcast_in_dim.32
  47.0 1.5 reshape.30
  48.5 0.7 constant_dynamic-slice_fusion.3
  49.2 84.1 %all-gather.10.cloned.1.call-done = f32[4,4,1024,128]{3,2,1,0:T(8,128)} async-done(((f32[1,4,1024,128]{3,2,1,0:T(8,128)}), f32[4,4,1024,128]{3,2,1,0:T(8,128)}) %all-gather.10.cloned.1.call-update) | async-done | bytes 8388624 | tf_op jit(solution)/shard_map/all_gather | solution.py:10
  133.3 4.1 reduce_sum.29
  137.5 0.2 copy.40
  137.7 1.1 multiply_convert_fusion.1
  138.9 0.2 copy.27
  139.0 4.7 broadcast_in_dim.31
  143.7 41.7 %while.24 = (s32[]{:T(128)}, f32[5120,4,128]{2,0,1:T(8,128)}, bf16[4,1024,5120]{2,1,0:T(8,128)(2,1)}, bf16[1,1024,128]{2,1,0:T(8,128)(2,1)S(1)}, s32[]{:T(128)}, /*index=5*/s32[]{:T(128)}, s32[]{:T(128)}) while((s32[]{:T(128)}, f32[5120,4,128]{2,0,1:T(8,128)}, bf16[4,1024,5120]{2,1,0:T(8,128)(2,1)}, bf16[1,1024,128]{2,1,0:T(8,128)(2,1)S(1)}, ...), condition=%wide.region_2.3_spmd, body=%wide.region_1.2_spmd.sunk | while | flops 1342832640 | bytes 21234804 | solution.py:20
  143.7 1.9 constant_dynamic-slice_fusion.8
  145.6 8.5 %fusion.61 = f32[5120,4,128]{2,0,1:T(8,128)} fusion(f32[5120,4,128]{2,0,1:T(8,128)} %get-tuple-element.241, s32[]{:T(128)S(6)} %select_n.50, bf16[4,1024,5120]{2,1,0:T(8,128)(2,1)} %get-tuple-element.249, f32[5120,1,128]{2,0,1:T(8,128)S(1)} %constant_dynamic-slice_fusion.8, bf16[1,1024,128]{2,1,0:T(8,128)(2,1)S(1)} %get-tuple-element.250), kind=kOutput, calls=%fused_computation.5.clone.1 | convolution fusion | flops 1342832640 | bytes 15991808 | tf_op jit(solution)/shard_map/while/body/dot_general | solution.py:66
  154.1 1.9 constant_dynamic-slice_fusion.8
  156.0 8.5 %fusion.61 = f32[5120,4,128]{2,0,1:T(8,128)} fusion(f32[5120,4,128]{2,0,1:T(8,128)} %get-tuple-element.241, s32[]{:T(128)S(6)} %select_n.50, bf16[4,1024,5120]{2,1,0:T(8,128)(2,1)} %get-tuple-element.249, f32[5120,1,128]{2,0,1:T(8,128)S(1)} %constant_dynamic-slice_fusion.8, bf16[1,1024,128]{2,1,0:T(8,128)(2,1)S(1)} %get-tuple-element.250), kind=kOutput, calls=%fused_computation.5.clone.1 | convolution fusion | flops 1342832640 | bytes 15991808 | tf_op jit(solution)/shard_map/while/body/dot_general | solution.py:66
  164.5 1.9 constant_dynamic-slice_fusion.8
  166.5 8.5 %fusion.61 = f32[5120,4,128]{2,0,1:T(8,128)} fusion(f32[5120,4,128]{2,0,1:T(8,128)} %get-tuple-element.241, s32[]{:T(128)S(6)} %select_n.50, bf16[4,1024,5120]{2,1,0:T(8,128)(2,1)} %get-tuple-element.249, f32[5120,1,128]{2,0,1:T(8,128)S(1)} %constant_dynamic-slice_fusion.8, bf16[1,1024,128]{2,1,0:T(8,128)(2,1)S(1)} %get-tuple-element.250), kind=kOutput, calls=%fused_computation.5.clone.1 | convolution fusion | flops 1342832640 | bytes 15991808 | tf_op jit(solution)/shard_map/while/body/dot_general | solution.py:66
  174.9 1.9 constant_dynamic-slice_fusion.8
  176.8 8.6 %fusion.61 = f32[5120,4,128]{2,0,1:T(8,128)} fusion(f32[5120,4,128]{2,0,1:T(8,128)} %get-tuple-element.241, s32[]{:T(128)S(6)} %select_n.50, bf16[4,1024,5120]{2,1,0:T(8,128)(2,1)} %get-tuple-element.249, f32[5120,1,128]{2,0,1:T(8,128)S(1)} %constant_dynamic-slice_fusion.8, bf16[1,1024,128]{2,1,0:T(8,128)(2,1)S(1)} %get-tuple-element.250), kind=kOutput, calls=%fused_computation.5.clone.1 | convolution fusion | flops 1342832640 | bytes 15991808 | tf_op jit(solution)/shard_map/while/body/dot_general | solution.py:66
  185.4 0.0 reduce-scatter.3.cloned.1.call-update
  185.4 0.0 all-gather.14.cloned.1.call-start
  185.5 108.5 %reduce-scatter.3.cloned.1.call-done = f32[640,4,128]{2,0,1:T(8,128)} async-done(((f32[5120,4,128]{2,0,1:T(8,128)}), f32[640,4,128]{2,0,1:T(8,128)}) %reduce-scatter.3.cloned.1.call-update) | async-done | bytes 1310736 | tf_op jit(solution)/shard_map/reduce_scatter | solution.py:76
  294.0 0.0 all-gather.14.cloned.1.call-update
  294.0 0.0 all-gather.16.cloned.1.call-start
  294.1 61.4 %all-gather.14.cloned.1.call-done = f32[2560,4,128]{2,0,1:T(8,128)} async-done(((f32[640,4,128]{2,0,1:T(8,128)}), f32[2560,4,128]{2,0,1:T(8,128)}) %all-gather.14.cloned.1.call-update) | async-done | bytes 5242896 | tf_op jit(solution)/shard_map/all_gather | solution.py:10
  355.5 3.0 reduce.1
  358.5 0.4 fusion.43
  358.9 1.3 copy.29
  360.3 0.0 all-gather.16.cloned.1.call-update
  360.3 0.2 all-gather.18.cloned.1.call-start
  360.5 55.9 %all-gather.16.cloned.1.call-done = bf16[1,5120,4,128]{3,2,0,1:T(4,128)(2,1)} async-done(((bf16[1,640,4,128]{3,2,0,1:T(4,128)(2,1)}), bf16[1,5120,4,128]{3,2,0,1:T(4,128)(2,1)}) %all-gather.16.cloned.1.call-update) | async-done | bytes 5242896 | tf_op jit(solution)/shard_map/all_gather | solution.py:98
  416.4 5.5 copy.31
  421.9 0.1 broadcast.17.clone
  422.0 24.3 %while.25 = (s32[]{:T(128)}, f32[4,1024,128]{2,1,0:T(8,128)S(1)}, s32[]{:T(128)}, bf16[4,1024,5120]{2,1,0:T(8,128)(2,1)}, bf16[5120,4,128]{2,0,1:T(8,128)(2,1)}, /*index=5*/s32[]{:T(128)}, s32[]{:T(128)}, s32[]{:T(128)}) while((s32[]{:T(128)}, f32[4,1024,128]{2,1,0:T(8,128)S(1)}, s32[]{:T(128)}, bf16[4,1024,5120]{2,1,0:T(8,128)(2,1)}, ...), condition=%wide.region_6.7_spmd, body=%wide.region_5.6_spmd.sunk | while | flops 1342308352 | bytes 13895291 | solution.py:20
  422.1 6.0 %fusion.64 = f32[4,1024,128]{2,1,0:T(8,128)S(1)} fusion(f32[4,1024,128]{2,1,0:T(8,128)S(1)} %get-tuple-element.263, s32[]{:T(128)} %get-tuple-element.272, bf16[5120,4,128]{2,0,1:T(8,128)(2,1)} %get-tuple-element.274, s32[]{:T(128)S(6)} %select_n.51, bf16[4,1024,5120]{2,1,0:T(8,128)(2,1)} %get-tuple-element.273, ...), kind=kOutput, calls=%fused_computation.16.clone.1 | convolution fusion | flops 1342308352 | bytes 12846592 | tf_op jit(solution)/shard_map/while/body/dot_general | solution.py:90
  428.2 6.0 %fusion.64 = f32[4,1024,128]{2,1,0:T(8,128)S(1)} fusion(f32[4,1024,128]{2,1,0:T(8,128)S(1)} %get-tuple-element.263, s32[]{:T(128)} %get-tuple-element.272, bf16[5120,4,128]{2,0,1:T(8,128)(2,1)} %get-tuple-element.274, s32[]{:T(128)S(6)} %select_n.51, bf16[4,1024,5120]{2,1,0:T(8,128)(2,1)} %get-tuple-element.273, ...), kind=kOutput, calls=%fused_computation.16.clone.1 | convolution fusion | flops 1342308352 | bytes 12846592 | tf_op jit(solution)/shard_map/while/body/dot_general | solution.py:90
  434.3 6.0 %fusion.64 = f32[4,1024,128]{2,1,0:T(8,128)S(1)} fusion(f32[4,1024,128]{2,1,0:T(8,128)S(1)} %get-tuple-element.263, s32[]{:T(128)} %get-tuple-element.272, bf16[5120,4,128]{2,0,1:T(8,128)(2,1)} %get-tuple-element.274, s32[]{:T(128)S(6)} %select_n.51, bf16[4,1024,5120]{2,1,0:T(8,128)(2,1)} %get-tuple-element.273, ...), kind=kOutput, calls=%fused_computation.16.clone.1 | convolution fusion | flops 1342308352 | bytes 12846592 | tf_op jit(solution)/shard_map/while/body/dot_general | solution.py:90
  440.4 6.0 %fusion.64 = f32[4,1024,128]{2,1,0:T(8,128)S(1)} fusion(f32[4,1024,128]{2,1,0:T(8,128)S(1)} %get-tuple-element.263, s32[]{:T(128)} %get-tuple-element.272, bf16[5120,4,128]{2,0,1:T(8,128)(2,1)} %get-tuple-element.274, s32[]{:T(128)S(6)} %select_n.51, bf16[4,1024,5120]{2,1,0:T(8,128)(2,1)} %get-tuple-element.273, ...), kind=kOutput, calls=%fused_computation.16.clone.1 | convolution fusion | flops 1342308352 | bytes 12846592 | tf_op jit(solution)/shard_map/while/body/dot_general | solution.py:90
  446.4 1.4 copy-done.2
  447.7 0.0 all-gather.18.cloned.1.call-update
  447.8 0.0 reduce-scatter.5.cloned.1.call-start
  447.8 84.5 %all-gather.18.cloned.1.call-done = f32[16,1024,128]{2,1,0:T(8,128)} async-done(((f32[4,1024,128]{2,1,0:T(8,128)}), f32[16,1024,128]{2,1,0:T(8,128)}) %all-gather.18.cloned.1.call-update) | async-done | bytes 8388624 | tf_op jit(solution)/shard_map/all_gather | solution.py:10
  532.3 4.1 reduce_sum.32
  536.5 0.2 copy.36
  536.7 7.3 %fusion.39 = f32[5120,128]{0,1:T(8,128)} fusion(bf16[1,1024,5120]{2,1,0:T(8,128)(2,1)} %param.12, f32[1,1024,128]{1,2,0:T(8,128)S(1)} %copy.36, f32[4,1024,128]{1,2,0:T(8,128)} %reshape.30, s32[]{:T(128)} %select_n.47), kind=kOutput, calls=%fused_computation.23 | convolution fusion | flops 1342439424 | bytes 14156288 | tf_op jit(solution)/shard_map/dot_general | solution.py:104
  544.0 0.0 reduce-scatter.5.cloned.1.call-update
  544.0 1.3 copy.33
  545.4 36.6 %reduce-scatter.5.cloned.1.call-done = f32[640,128]{0,1:T(8,128)} async-done(((f32[5120,128]{0,1:T(8,128)}), f32[640,128]{0,1:T(8,128)}) %reduce-scatter.5.cloned.1.call-update) | async-done | bytes 327696 | tf_op jit(solution)/shard_map/reduce_scatter | solution.py:103
  582.0 1.0 convert_bitcast_fusion
  583.0 0.8 copy.34
  (17 shorter events, 0.3 us)
Async XLA Ops:
  7.2 1.1 copy-start
  7.2 29.2 %all-gather.12.cloned.1.call-start = ((), (), s32[]{:S(2)}) async-start(), calls=%async_computation.5 | async-start | bytes 1474560 | tf_op jit(solution)/shard_map/all_gather | solution.py:49
  9.0 124.4 %all-gather.10.cloned.1.call-start = ((), (), s32[]{:S(2)}) async-start(), calls=%async_computation.2 | async-start | bytes 10485760 | tf_op jit(solution)/shard_map/all_gather | solution.py:10
  44.6 1.7 copy-start.5
  44.8 1.4 copy-start.3
  46.2 247.8 %reduce-scatter.3.cloned.1.call-start = ((), (), s32[]{:S(2)}) async-start(), calls=%async_computation.3 | async-start | bytes 11796480 | tf_op jit(solution)/shard_map/reduce_scatter | solution.py:76
  185.4 170.1 %all-gather.14.cloned.1.call-start = ((), (), s32[]{:S(2)}) async-start(), calls=%async_computation.6 | async-start | bytes 6553600 | tf_op jit(solution)/shard_map/all_gather | solution.py:10
  294.0 122.4 %all-gather.16.cloned.1.call-start = ((), (), s32[]{:S(2)}) async-start(), calls=%async_computation.7 | async-start | bytes 5898240 | tf_op jit(solution)/shard_map/all_gather | solution.py:98
  355.5 3.0 copy-start.4
  355.5 3.0 copy-start.6
  360.3 172.1 %all-gather.18.cloned.1.call-start = ((), (), s32[]{:S(2)}) async-start(), calls=%async_computation.8 | async-start | bytes 10485760 | tf_op jit(solution)/shard_map/all_gather | solution.py:10
  446.4 1.4 copy-start.2
  447.8 134.2 %reduce-scatter.5.cloned.1.call-start = ((), (), s32[]{:S(2)}) async-start(), calls=%async_computation.4 | async-start | bytes 2949120 | tf_op jit(solution)/shard_map/reduce_scatter | solution.py:103
  536.7 47.1 %copy-start.1 = (bf16[4,1,640,128]{3,2,1,0:T(8,128)(2,1)S(1)}, bf16[4,1,640,128]{3,2,1,0:T(8,128)(2,1)}, u32[]{:S(2)}) copy-start(bf16[4,1,640,128]{3,2,1,0:T(8,128)(2,1)} %param.11) | copy-start | bytes 1966084
Sparse Core Ops, SparseCore 0:
  10.2 26.1 all-gather.11
  46.3 86.9 all-gather.9
  185.5 108.4 reduce-scatter.2
  295.7 59.7 all-gather.13
  360.4 55.9 all-gather.15
  447.9 84.4 all-gather.17
  544.1 37.7 reduce-scatter.4
